TPU v7x, 32 devices: a whole 2x2x4 slice. The times are simulated.
32 devices in a mesh: gx: 4 (over y, core), gy: 2 (over x), gz: 4 (over z).
Axes of the slice: x: 2, y: 2, z: 4, core: 2. Of those that a mesh axis runs over, the one named last changes fastest.
Arguments:
- dual_ops: bfloat16 [4, 2, 4, 768, 768], P('gx', 'gy', 'gz'), may hold values from -1 to 1, as said below
- schur_ops: bfloat16 [4, 2, 4, 768, 768], P('gx', 'gy', 'gz'), may hold values from -1 to 1, as said below
- local_rhs: float32 [4, 2, 4, 768, 128], P('gx', 'gy', 'gz'), may hold values from -6 to 6
- ordering: int32 [4, 2, 4, 768], P('gx', 'gy', 'gz'), may hold values from 0 to 127, as said below
- intact: int32 [4, 2, 4, 768], P('gx', 'gy', 'gz'), may hold values from 0 to 1, as said below
Outputs:
- multipliers: float32 [4, 2, 4, 768, 128], P('gx', 'gy', 'gz')
Inputs may be any that keep to these rules, and one draw needn't show every extreme that they name: `ordering`: for every subdomain and face, the 128 entries of that face form a permutation of 0 .. 127. `intact`: an entry of face -x (or -y, -z) of a subdomain equals the entry of the same shared index on face +x (+y, +z) of its cyclic neighbour across that face. `dual_ops`: each block is symmetric positive definite. `schur_ops`: each block is symmetric positive definite.
All inputs are finite; a program needn't handle non-finite values.
Results may differ from a plain program's by a relative error of at most 0.0047.
Values may be sent and summed in bfloat16 or wider, within the bound.
A program may use at most 64 MiB of HBM per device.

v0:
```python
import jax
import jax.numpy as jnp
from jax import lax
from jax.sharding import PartitionSpec as P

FM = 128
ITERS = 4


def padded(cells, sides, width):
    for axis, dim in sides:
        count = lax.axis_size(axis)
        head = lax.slice_in_dim(cells, 0, width, axis=dim)
        tail = lax.slice_in_dim(cells, cells.shape[dim] - width, cells.shape[dim], axis=dim)
        cells = jnp.concatenate(
            [
                lax.ppermute(tail, axis, [(i, (i + 1) % count) for i in range(count)]),
                cells,
                lax.ppermute(head, axis, [((i + 1) % count, i) for i in range(count)]),
            ],
            axis=dim,
        )
    return cells


def to_shared(block, onehot_half):
    moved = jnp.einsum("fkc,fkl->fcl", onehot_half, block, preferred_element_type=jnp.float32)
    return moved.astype(jnp.bfloat16)


def assemble(partial_fn, onehot_half, keep_local):
    z_part = partial_fn(4, 2)
    z_shared = to_shared(z_part, onehot_half[4:6])
    along_z = padded(z_shared, (("gz", 0),), 1)
    xy_part = partial_fn(0, 4)
    xy_shared = to_shared(xy_part, onehot_half[0:4])
    own_part = jnp.concatenate([xy_part, z_part], axis=0)
    own_shared = jnp.concatenate([xy_shared, z_shared], axis=0)
    along_x = padded(own_shared[0:2], (("gx", 0),), 1)
    along_y = padded(own_shared[2:4], (("gy", 0),), 1)
    across = jnp.stack(
        [along_x[0], along_x[3], along_y[0], along_y[3], along_z[0], along_z[3]], axis=0
    )
    across_local = jnp.einsum(
        "fkc,fcl->fkl", onehot_half, across, preferred_element_type=jnp.float32
    )
    total = (own_part.astype(jnp.float32) + across_local) * keep_local
    return total.reshape(6 * FM, total.shape[2])


def local(dual_ops, schur_ops, local_rhs, ordering, intact):
    dual = dual_ops[0, 0, 0]
    schur = schur_ops[0, 0, 0]
    rhs = local_rhs[0, 0, 0]
    loads = rhs.shape[1]
    order = ordering[0, 0, 0].reshape(6, FM)
    keep_shared = intact[0, 0, 0].reshape(6, 1, FM).astype(jnp.float32)
    matches = order[:, :, None] == jnp.arange(FM, dtype=jnp.int32)[None, None, :]
    onehot_half = matches.astype(jnp.bfloat16)
    keep_local = jnp.sum(jnp.where(matches, keep_shared, 0.0), axis=2)[:, :, None]
    low, high = (0.2, 2.5)
    theta = (high + low) / 2.0
    delta = (high - low) / 2.0
    sigma = theta / delta
    rho = 1.0 / sigma
    multipliers = jnp.zeros((6 * FM, loads), jnp.float32)
    update = jnp.zeros((6 * FM, loads), jnp.float32)
    for step in range(ITERS):
        if step == 0:

            def rhs_part(first, count):
                rows = rhs[first * FM : (first + count) * FM]
                return rows.astype(jnp.bfloat16).reshape(count, FM, loads)

            residual = assemble(rhs_part, onehot_half, keep_local)
        else:
            mult_half = multipliers.astype(jnp.bfloat16)

            def dual_part(first, count):
                rows = dual[first * FM : (first + count) * FM]
                product = jnp.dot(rows, mult_half, preferred_element_type=jnp.float32)
                value = rhs[first * FM : (first + count) * FM] - product
                return value.astype(jnp.bfloat16).reshape(count, FM, loads)

            residual = assemble(dual_part, onehot_half, keep_local)
        res_half = residual.astype(jnp.bfloat16)

        def schur_part(first, count):
            rows = schur[first * FM : (first + count) * FM]
            product = jnp.dot(rows, res_half, preferred_element_type=jnp.float32)
            return product.astype(jnp.bfloat16).reshape(count, FM, loads)

        precond = assemble(schur_part, onehot_half, keep_local)
        if step == 0:
            update = precond / theta
        else:
            rho_new = 1.0 / (2.0 * sigma - rho)
            update = rho_new * rho * update + 2.0 * rho_new / delta * precond
            rho = rho_new
        multipliers = multipliers + update
    return multipliers.reshape(1, 1, 1, 6 * FM, loads)


def solution(mesh):
    in_specs = (
        P("gx", "gy", "gz", None, None),
        P("gx", "gy", "gz", None, None),
        P("gx", "gy", "gz", None, None),
        P("gx", "gy", "gz", None),
        P("gx", "gy", "gz", None),
    )
    out_specs = P("gx", "gy", "gz", None, None)
    return jax.shard_map(local, mesh=mesh, in_specs=in_specs, out_specs=out_specs, check_vma=False)
```

profile of v0, /device:TPU:0, one launch (start us, length us, event | category | flops | bytes accessed | tf_op | source)
XLA Modules:
  0.0 93.8 jit_solution(13525419666240028932)
XLA Ops:
  2.1 5.1 %collective-permute-start.5 = (bf16[1,128,128]{2,1,0:T(8,128)(2,1)S(1)}, bf16[1,128,128]{2,1,0:T(8,128)(2,1)S(1)}, u32[]{:S(2)}, u32[]{:S(2)}) collective-permute-start(bf16[1,128,128]{2,1,0:T(8,128)(2,1)S(1)} %get-tuple-element.51), channel_id=1, source_target_pairs={{1,0},{2,1},{3,2},{0,3},{5,4},{6,5},{7,6},{4,7},{9,8},{10,9},{11,1... | collective-permute-start | bytes 98312 | tf_op jit(solution)/shard_map/ppermute | solution.py:19
  7.7 1.6 %collective-permute-start.3 = (bf16[1,128,128]{2,1,0:T(8,128)(2,1)S(1)}, bf16[1,128,128]{2,1,0:T(8,128)(2,1)S(1)}, u32[]{:S(2)}, u32[]{:S(2)}) collective-permute-start(bf16[1,128,128]{2,1,0:T(8,128)(2,1)S(1)} %get-tuple-element.33), channel_id=1, source_target_pairs={{4,0},{0,4},{5,1},{1,5},{6,2},{2,6},{7,3},{3,7},{12,8},{8,12},{13,... | collective-permute-start | bytes 98312 | tf_op jit(solution)/shard_map/ppermute | solution.py:19
  10.0 3.1 %collective-permute-done = bf16[1,128,128]{2,1,0:T(8,128)(2,1)S(1)} collective-permute-done((bf16[1,128,128]{2,1,0:T(8,128)(2,1)S(1)}, bf16[1,128,128]{2,1,0:T(8,128)(2,1)S(1)}, u32[]{:S(2)}, u32[]{:S(2)}) %collective-permute-start) | collective-permute-done | bytes 32800 | tf_op jit(solution)/shard_map/ppermute | solution.py:17
  13.2 1.6 %collective-permute-done.1 = bf16[1,128,128]{2,1,0:T(8,128)(2,1)S(1)} collective-permute-done((bf16[1,128,128]{2,1,0:T(8,128)(2,1)S(1)}, bf16[1,128,128]{2,1,0:T(8,128)(2,1)S(1)}, u32[]{:S(2)}, u32[]{:S(2)}) %collective-permute-start.1) | collective-permute-done | bytes 32800 | tf_op jit(solution)/shard_map/ppermute | solution.py:19
  16.5 1.7 %collective-permute-start.6 = (bf16[1,128,128]{2,1,0:T(8,128)(2,1)S(1)}, bf16[1,128,128]{2,1,0:T(8,128)(2,1)S(1)}, u32[]{:S(2)}, u32[]{:S(2)}) collective-permute-start(bf16[1,128,128]{2,1,0:T(8,128)(2,1)S(1)} %get-tuple-element.32), channel_id=1, source_target_pairs={{0,8},{8,16},{16,24},{24,0},{1,9},{9,17},{17,25},{25,1},{2,10},{10... | collective-permute-start | bytes 98312 | tf_op jit(solution)/shard_map/ppermute | solution.py:17
  18.2 3.8 %collective-permute-start.11 = (bf16[1,128,128]{2,1,0:T(8,128)(2,1)S(1)}, bf16[1,128,128]{2,1,0:T(8,128)(2,1)S(1)}, u32[]{:S(2)}, u32[]{:S(2)}) collective-permute-start(bf16[1,128,128]{2,1,0:T(8,128)(2,1)S(1)} %get-tuple-element.49), channel_id=1, source_target_pairs={{1,0},{2,1},{3,2},{0,3},{5,4},{6,5},{7,6},{4,7},{9,8},{10,9},{11,1... | collective-permute-start | bytes 98312 | tf_op jit(solution)/shard_map/ppermute | solution.py:19
  22.0 1.5 %collective-permute-start.9 = (bf16[1,128,128]{2,1,0:T(8,128)(2,1)S(1)}, bf16[1,128,128]{2,1,0:T(8,128)(2,1)S(1)}, u32[]{:S(2)}, u32[]{:S(2)}) collective-permute-start(bf16[1,128,128]{2,1,0:T(8,128)(2,1)S(1)} %get-tuple-element.29), channel_id=1, source_target_pairs={{4,0},{0,4},{5,1},{1,5},{6,2},{2,6},{7,3},{3,7},{12,8},{8,12},{13,... | collective-permute-start | bytes 98312 | tf_op jit(solution)/shard_map/ppermute | solution.py:19
  24.1 1.6 %collective-permute-done.7 = bf16[1,128,128]{2,1,0:T(8,128)(2,1)S(1)} collective-permute-done((bf16[1,128,128]{2,1,0:T(8,128)(2,1)S(1)}, bf16[1,128,128]{2,1,0:T(8,128)(2,1)S(1)}, u32[]{:S(2)}, u32[]{:S(2)}) %collective-permute-start.7) | collective-permute-done | bytes 32800 | tf_op jit(solution)/shard_map/ppermute | solution.py:19
  25.7 1.8 %collective-permute-done.8 = bf16[1,128,128]{2,1,0:T(8,128)(2,1)S(1)} collective-permute-done((bf16[1,128,128]{2,1,0:T(8,128)(2,1)S(1)}, bf16[1,128,128]{2,1,0:T(8,128)(2,1)S(1)}, u32[]{:S(2)}, u32[]{:S(2)}) %collective-permute-start.8) | collective-permute-done | bytes 32800 | tf_op jit(solution)/shard_map/ppermute | solution.py:17
  29.5 3.6 %collective-permute-start.17 = (bf16[1,128,128]{2,1,0:T(8,128)(2,1)S(1)}, bf16[1,128,128]{2,1,0:T(8,128)(2,1)S(1)}, u32[]{:S(2)}, u32[]{:S(2)}) collective-permute-start(bf16[1,128,128]{2,1,0:T(8,128)(2,1)S(1)} %get-tuple-element.47), channel_id=1, source_target_pairs={{1,0},{2,1},{3,2},{0,3},{5,4},{6,5},{7,6},{4,7},{9,8},{10,9},{11,1... | collective-permute-start | bytes 98312 | tf_op jit(solution)/shard_map/ppermute | solution.py:19
  33.7 1.4 %collective-permute-start.14 = (bf16[1,128,128]{2,1,0:T(8,128)(2,1)S(1)}, bf16[1,128,128]{2,1,0:T(8,128)(2,1)S(1)}, u32[]{:S(2)}, u32[]{:S(2)}) collective-permute-start(bf16[1,128,128]{2,1,0:T(8,128)(2,1)S(1)} %get-tuple-element.26), channel_id=1, source_target_pairs={{0,4},{4,0},{1,5},{5,1},{2,6},{6,2},{3,7},{7,3},{8,12},{12,8},{9,1... | collective-permute-start | bytes 98312 | tf_op jit(solution)/shard_map/ppermute | solution.py:17
  36.0 1.6 %collective-permute-done.13 = bf16[1,128,128]{2,1,0:T(8,128)(2,1)S(1)} collective-permute-done((bf16[1,128,128]{2,1,0:T(8,128)(2,1)S(1)}, bf16[1,128,128]{2,1,0:T(8,128)(2,1)S(1)}, u32[]{:S(2)}, u32[]{:S(2)}) %collective-permute-start.13) | collective-permute-done | bytes 32800 | tf_op jit(solution)/shard_map/ppermute | solution.py:19
  40.6 3.0 %collective-permute-start.23 = (bf16[1,128,128]{2,1,0:T(8,128)(2,1)S(1)}, bf16[1,128,128]{2,1,0:T(8,128)(2,1)S(1)}, u32[]{:S(2)}, u32[]{:S(2)}) collective-permute-start(bf16[1,128,128]{2,1,0:T(8,128)(2,1)S(1)} %get-tuple-element.45), channel_id=1, source_target_pairs={{1,0},{2,1},{3,2},{0,3},{5,4},{6,5},{7,6},{4,7},{9,8},{10,9},{11,1... | collective-permute-start | bytes 98312 | tf_op jit(solution)/shard_map/ppermute | solution.py:19
  46.2 1.6 %collective-permute-done.19 = bf16[1,128,128]{2,1,0:T(8,128)(2,1)S(1)} collective-permute-done((bf16[1,128,128]{2,1,0:T(8,128)(2,1)S(1)}, bf16[1,128,128]{2,1,0:T(8,128)(2,1)S(1)}, u32[]{:S(2)}, u32[]{:S(2)}) %collective-permute-start.19) | collective-permute-done | bytes 32800 | tf_op jit(solution)/shard_map/ppermute | solution.py:19
  51.3 3.2 %collective-permute-start.29 = (bf16[1,128,128]{2,1,0:T(8,128)(2,1)S(1)}, bf16[1,128,128]{2,1,0:T(8,128)(2,1)S(1)}, u32[]{:S(2)}, u32[]{:S(2)}) collective-permute-start(bf16[1,128,128]{2,1,0:T(8,128)(2,1)S(1)} %get-tuple-element.43), channel_id=1, source_target_pairs={{1,0},{2,1},{3,2},{0,3},{5,4},{6,5},{7,6},{4,7},{9,8},{10,9},{11,1... | collective-permute-start | bytes 98312 | tf_op jit(solution)/shard_map/ppermute | solution.py:19
  57.3 1.6 %collective-permute-done.25 = bf16[1,128,128]{2,1,0:T(8,128)(2,1)S(1)} collective-permute-done((bf16[1,128,128]{2,1,0:T(8,128)(2,1)S(1)}, bf16[1,128,128]{2,1,0:T(8,128)(2,1)S(1)}, u32[]{:S(2)}, u32[]{:S(2)}) %collective-permute-start.25) | collective-permute-done | bytes 32800 | tf_op jit(solution)/shard_map/ppermute | solution.py:19
  62.1 3.2 %collective-permute-start.35 = (bf16[1,128,128]{2,1,0:T(8,128)(2,1)S(1)}, bf16[1,128,128]{2,1,0:T(8,128)(2,1)S(1)}, u32[]{:S(2)}, u32[]{:S(2)}) collective-permute-start(bf16[1,128,128]{2,1,0:T(8,128)(2,1)S(1)} %get-tuple-element.41), channel_id=1, source_target_pairs={{1,0},{2,1},{3,2},{0,3},{5,4},{6,5},{7,6},{4,7},{9,8},{10,9},{11,1... | collective-permute-start | bytes 98312 | tf_op jit(solution)/shard_map/ppermute | solution.py:19
  65.3 1.4 %collective-permute-start.33 = (bf16[1,128,128]{2,1,0:T(8,128)(2,1)S(1)}, bf16[1,128,128]{2,1,0:T(8,128)(2,1)S(1)}, u32[]{:S(2)}, u32[]{:S(2)}) collective-permute-start(bf16[1,128,128]{2,1,0:T(8,128)(2,1)S(1)} %get-tuple-element.13), channel_id=1, source_target_pairs={{4,0},{0,4},{5,1},{1,5},{6,2},{2,6},{7,3},{3,7},{12,8},{8,12},{13,... | collective-permute-start | bytes 98312 | tf_op jit(solution)/shard_map/ppermute | solution.py:19
  67.8 1.6 %collective-permute-done.31 = bf16[1,128,128]{2,1,0:T(8,128)(2,1)S(1)} collective-permute-done((bf16[1,128,128]{2,1,0:T(8,128)(2,1)S(1)}, bf16[1,128,128]{2,1,0:T(8,128)(2,1)S(1)}, u32[]{:S(2)}, u32[]{:S(2)}) %collective-permute-start.31) | collective-permute-done | bytes 32800 | tf_op jit(solution)/shard_map/ppermute | solution.py:19
  73.2 3.3 %collective-permute-start.41 = (bf16[1,128,128]{2,1,0:T(8,128)(2,1)S(1)}, bf16[1,128,128]{2,1,0:T(8,128)(2,1)S(1)}, u32[]{:S(2)}, u32[]{:S(2)}) collective-permute-start(bf16[1,128,128]{2,1,0:T(8,128)(2,1)S(1)} %get-tuple-element.39), channel_id=1, source_target_pairs={{1,0},{2,1},{3,2},{0,3},{5,4},{6,5},{7,6},{4,7},{9,8},{10,9},{11,1... | collective-permute-start | bytes 98312 | tf_op jit(solution)/shard_map/ppermute | solution.py:19
  77.1 1.3 %collective-permute-start.38 = (bf16[1,128,128]{2,1,0:T(8,128)(2,1)S(1)}, bf16[1,128,128]{2,1,0:T(8,128)(2,1)S(1)}, u32[]{:S(2)}, u32[]{:S(2)}) collective-permute-start(bf16[1,128,128]{2,1,0:T(8,128)(2,1)S(1)} %get-tuple-element.10), channel_id=1, source_target_pairs={{0,4},{4,0},{1,5},{5,1},{2,6},{6,2},{3,7},{7,3},{8,12},{12,8},{9,1... | collective-permute-start | bytes 98312 | tf_op jit(solution)/shard_map/ppermute | solution.py:17
  79.2 1.6 %collective-permute-done.37 = bf16[1,128,128]{2,1,0:T(8,128)(2,1)S(1)} collective-permute-done((bf16[1,128,128]{2,1,0:T(8,128)(2,1)S(1)}, bf16[1,128,128]{2,1,0:T(8,128)(2,1)S(1)}, u32[]{:S(2)}, u32[]{:S(2)}) %collective-permute-start.37) | collective-permute-done | bytes 32800 | tf_op jit(solution)/shard_map/ppermute | solution.py:19
  83.9 2.9 %collective-permute-start.47 = (bf16[1,128,128]{2,1,0:T(8,128)(2,1)S(1)}, bf16[1,128,128]{2,1,0:T(8,128)(2,1)S(1)}, u32[]{:S(2)}, u32[]{:S(2)}) collective-permute-start(bf16[1,128,128]{2,1,0:T(8,128)(2,1)S(1)} %get-tuple-element.37), channel_id=1, source_target_pairs={{1,0},{2,1},{3,2},{0,3},{5,4},{6,5},{7,6},{4,7},{9,8},{10,9},{11,1... | collective-permute-start | bytes 98312 | tf_op jit(solution)/shard_map/ppermute | solution.py:19
  89.6 1.6 %collective-permute-done.43 = bf16[1,128,128]{2,1,0:T(8,128)(2,1)S(1)} collective-permute-done((bf16[1,128,128]{2,1,0:T(8,128)(2,1)S(1)}, bf16[1,128,128]{2,1,0:T(8,128)(2,1)S(1)}, u32[]{:S(2)}, u32[]{:S(2)}) %collective-permute-start.43) | collective-permute-done | bytes 32800 | tf_op jit(solution)/shard_map/ppermute | solution.py:19
  (212 shorter events, 38.3 us)
Async XLA Ops:
  2.1 12.8 %collective-permute-start.5 = (bf16[1,128,128]{2,1,0:T(8,128)(2,1)S(1)}, bf16[1,128,128]{2,1,0:T(8,128)(2,1)S(1)}, u32[]{:S(2)}, u32[]{:S(2)}) collective-permute-start(bf16[1,128,128]{2,1,0:T(8,128)(2,1)S(1)} %get-tuple-element.51), channel_id=1, source_target_pairs={{1,0},{2,1},{3,2},{0,3},{5,4},{6,5},{7,6},{4,7},{9,8},{10,9},{11,1... | collective-permute-start | bytes 98312 | tf_op jit(solution)/shard_map/ppermute | solution.py:19
  7.2 7.6 %collective-permute-start.4 = (bf16[1,128,128]{2,1,0:T(8,128)(2,1)S(1)}, bf16[1,128,128]{2,1,0:T(8,128)(2,1)S(1)}, u32[]{:S(2)}, u32[]{:S(2)}) collective-permute-start(bf16[1,128,128]{2,1,0:T(8,128)(2,1)S(1)} %get-tuple-element.52), channel_id=1, source_target_pairs={{0,1},{1,2},{2,3},{3,0},{4,5},{5,6},{6,7},{7,4},{8,9},{9,10},{10,1... | collective-permute-start | bytes 98312 | tf_op jit(solution)/shard_map/ppermute | solution.py:17
  7.7 7.1 %collective-permute-start.3 = (bf16[1,128,128]{2,1,0:T(8,128)(2,1)S(1)}, bf16[1,128,128]{2,1,0:T(8,128)(2,1)S(1)}, u32[]{:S(2)}, u32[]{:S(2)}) collective-permute-start(bf16[1,128,128]{2,1,0:T(8,128)(2,1)S(1)} %get-tuple-element.33), channel_id=1, source_target_pairs={{4,0},{0,4},{5,1},{1,5},{6,2},{2,6},{7,3},{3,7},{12,8},{8,12},{13,... | collective-permute-start | bytes 98312 | tf_op jit(solution)/shard_map/ppermute | solution.py:19
  9.3 5.5 %collective-permute-start.2 = (bf16[1,128,128]{2,1,0:T(8,128)(2,1)S(1)}, bf16[1,128,128]{2,1,0:T(8,128)(2,1)S(1)}, u32[]{:S(2)}, u32[]{:S(2)}) collective-permute-start(bf16[1,128,128]{2,1,0:T(8,128)(2,1)S(1)} %get-tuple-element.34), channel_id=1, source_target_pairs={{0,4},{4,0},{1,5},{5,1},{2,6},{6,2},{3,7},{7,3},{8,12},{12,8},{9,1... | collective-permute-start | bytes 98312 | tf_op jit(solution)/shard_map/ppermute | solution.py:17
  16.5 7.5 %collective-permute-start.6 = (bf16[1,128,128]{2,1,0:T(8,128)(2,1)S(1)}, bf16[1,128,128]{2,1,0:T(8,128)(2,1)S(1)}, u32[]{:S(2)}, u32[]{:S(2)}) collective-permute-start(bf16[1,128,128]{2,1,0:T(8,128)(2,1)S(1)} %get-tuple-element.32), channel_id=1, source_target_pairs={{0,8},{8,16},{16,24},{24,0},{1,9},{9,17},{17,25},{25,1},{2,10},{10... | collective-permute-start | bytes 98312 | tf_op jit(solution)/shard_map/ppermute | solution.py:17
  18.2 9.5 %collective-permute-start.11 = (bf16[1,128,128]{2,1,0:T(8,128)(2,1)S(1)}, bf16[1,128,128]{2,1,0:T(8,128)(2,1)S(1)}, u32[]{:S(2)}, u32[]{:S(2)}) collective-permute-start(bf16[1,128,128]{2,1,0:T(8,128)(2,1)S(1)} %get-tuple-element.49), channel_id=1, source_target_pairs={{1,0},{2,1},{3,2},{0,3},{5,4},{6,5},{7,6},{4,7},{9,8},{10,9},{11,1... | collective-permute-start | bytes 98312 | tf_op jit(solution)/shard_map/ppermute | solution.py:19
  22.0 5.7 %collective-permute-start.10 = (bf16[1,128,128]{2,1,0:T(8,128)(2,1)S(1)}, bf16[1,128,128]{2,1,0:T(8,128)(2,1)S(1)}, u32[]{:S(2)}, u32[]{:S(2)}) collective-permute-start(bf16[1,128,128]{2,1,0:T(8,128)(2,1)S(1)} %get-tuple-element.50), channel_id=1, source_target_pairs={{0,1},{1,2},{2,3},{3,0},{4,5},{5,6},{6,7},{7,4},{8,9},{9,10},{10,1... | collective-permute-start | bytes 98312 | tf_op jit(solution)/shard_map/ppermute | solution.py:17
  22.0 5.4 %collective-permute-start.9 = (bf16[1,128,128]{2,1,0:T(8,128)(2,1)S(1)}, bf16[1,128,128]{2,1,0:T(8,128)(2,1)S(1)}, u32[]{:S(2)}, u32[]{:S(2)}) collective-permute-start(bf16[1,128,128]{2,1,0:T(8,128)(2,1)S(1)} %get-tuple-element.29), channel_id=1, source_target_pairs={{4,0},{0,4},{5,1},{1,5},{6,2},{2,6},{7,3},{3,7},{12,8},{8,12},{13,... | collective-permute-start | bytes 98312 | tf_op jit(solution)/shard_map/ppermute | solution.py:19
  29.4 5.7 %collective-permute-start.12 = (bf16[1,128,128]{2,1,0:T(8,128)(2,1)S(1)}, bf16[1,128,128]{2,1,0:T(8,128)(2,1)S(1)}, u32[]{:S(2)}, u32[]{:S(2)}) collective-permute-start(bf16[1,128,128]{2,1,0:T(8,128)(2,1)S(1)} %get-tuple-element.28), channel_id=1, source_target_pairs={{0,8},{8,16},{16,24},{24,0},{1,9},{9,17},{17,25},{25,1},{2,10},{10... | collective-permute-start | bytes 98312 | tf_op jit(solution)/shard_map/ppermute | solution.py:17
  29.5 9.4 %collective-permute-start.17 = (bf16[1,128,128]{2,1,0:T(8,128)(2,1)S(1)}, bf16[1,128,128]{2,1,0:T(8,128)(2,1)S(1)}, u32[]{:S(2)}, u32[]{:S(2)}) collective-permute-start(bf16[1,128,128]{2,1,0:T(8,128)(2,1)S(1)} %get-tuple-element.47), channel_id=1, source_target_pairs={{1,0},{2,1},{3,2},{0,3},{5,4},{6,5},{7,6},{4,7},{9,8},{10,9},{11,1... | collective-permute-start | bytes 98312 | tf_op jit(solution)/shard_map/ppermute | solution.py:19
  33.1 5.7 %collective-permute-start.16 = (bf16[1,128,128]{2,1,0:T(8,128)(2,1)S(1)}, bf16[1,128,128]{2,1,0:T(8,128)(2,1)S(1)}, u32[]{:S(2)}, u32[]{:S(2)}) collective-permute-start(bf16[1,128,128]{2,1,0:T(8,128)(2,1)S(1)} %get-tuple-element.48), channel_id=1, source_target_pairs={{0,1},{1,2},{2,3},{3,0},{4,5},{5,6},{6,7},{7,4},{8,9},{9,10},{10,1... | collective-permute-start | bytes 98312 | tf_op jit(solution)/shard_map/ppermute | solution.py:17
  40.6 8.8 %collective-permute-start.23 = (bf16[1,128,128]{2,1,0:T(8,128)(2,1)S(1)}, bf16[1,128,128]{2,1,0:T(8,128)(2,1)S(1)}, u32[]{:S(2)}, u32[]{:S(2)}) collective-permute-start(bf16[1,128,128]{2,1,0:T(8,128)(2,1)S(1)} %get-tuple-element.45), channel_id=1, source_target_pairs={{1,0},{2,1},{3,2},{0,3},{5,4},{6,5},{7,6},{4,7},{9,8},{10,9},{11,1... | collective-permute-start | bytes 98312 | tf_op jit(solution)/shard_map/ppermute | solution.py:19
  43.6 5.8 %collective-permute-start.22 = (bf16[1,128,128]{2,1,0:T(8,128)(2,1)S(1)}, bf16[1,128,128]{2,1,0:T(8,128)(2,1)S(1)}, u32[]{:S(2)}, u32[]{:S(2)}) collective-permute-start(bf16[1,128,128]{2,1,0:T(8,128)(2,1)S(1)} %get-tuple-element.46), channel_id=1, source_target_pairs={{0,1},{1,2},{2,3},{3,0},{4,5},{5,6},{6,7},{7,4},{8,9},{9,10},{10,1... | collective-permute-start | bytes 98312 | tf_op jit(solution)/shard_map/ppermute | solution.py:17
  51.1 5.4 %collective-permute-start.24 = (bf16[1,128,128]{2,1,0:T(8,128)(2,1)S(1)}, bf16[1,128,128]{2,1,0:T(8,128)(2,1)S(1)}, u32[]{:S(2)}, u32[]{:S(2)}) collective-permute-start(bf16[1,128,128]{2,1,0:T(8,128)(2,1)S(1)} %get-tuple-element.20), channel_id=1, source_target_pairs={{0,8},{8,16},{16,24},{24,0},{1,9},{9,17},{17,25},{25,1},{2,10},{10... | collective-permute-start | bytes 98312 | tf_op jit(solution)/shard_map/ppermute | solution.py:17
  51.3 9.0 %collective-permute-start.29 = (bf16[1,128,128]{2,1,0:T(8,128)(2,1)S(1)}, bf16[1,128,128]{2,1,0:T(8,128)(2,1)S(1)}, u32[]{:S(2)}, u32[]{:S(2)}) collective-permute-start(bf16[1,128,128]{2,1,0:T(8,128)(2,1)S(1)} %get-tuple-element.43), channel_id=1, source_target_pairs={{1,0},{2,1},{3,2},{0,3},{5,4},{6,5},{7,6},{4,7},{9,8},{10,9},{11,1... | collective-permute-start | bytes 98312 | tf_op jit(solution)/shard_map/ppermute | solution.py:19
  54.5 5.7 %collective-permute-start.28 = (bf16[1,128,128]{2,1,0:T(8,128)(2,1)S(1)}, bf16[1,128,128]{2,1,0:T(8,128)(2,1)S(1)}, u32[]{:S(2)}, u32[]{:S(2)}) collective-permute-start(bf16[1,128,128]{2,1,0:T(8,128)(2,1)S(1)} %get-tuple-element.44), channel_id=1, source_target_pairs={{0,1},{1,2},{2,3},{3,0},{4,5},{5,6},{6,7},{7,4},{8,9},{9,10},{10,1... | collective-permute-start | bytes 98312 | tf_op jit(solution)/shard_map/ppermute | solution.py:17
  61.9 5.4 %collective-permute-start.30 = (bf16[1,128,128]{2,1,0:T(8,128)(2,1)S(1)}, bf16[1,128,128]{2,1,0:T(8,128)(2,1)S(1)}, u32[]{:S(2)}, u32[]{:S(2)}) collective-permute-start(bf16[1,128,128]{2,1,0:T(8,128)(2,1)S(1)} %get-tuple-element.16), channel_id=1, source_target_pairs={{0,8},{8,16},{16,24},{24,0},{1,9},{9,17},{17,25},{25,1},{2,10},{10... | collective-permute-start | bytes 98312 | tf_op jit(solution)/shard_map/ppermute | solution.py:17
  62.1 9.3 %collective-permute-start.35 = (bf16[1,128,128]{2,1,0:T(8,128)(2,1)S(1)}, bf16[1,128,128]{2,1,0:T(8,128)(2,1)S(1)}, u32[]{:S(2)}, u32[]{:S(2)}) collective-permute-start(bf16[1,128,128]{2,1,0:T(8,128)(2,1)S(1)} %get-tuple-element.41), channel_id=1, source_target_pairs={{1,0},{2,1},{3,2},{0,3},{5,4},{6,5},{7,6},{4,7},{9,8},{10,9},{11,1... | collective-permute-start | bytes 98312 | tf_op jit(solution)/shard_map/ppermute | solution.py:19
  65.3 6.0 %collective-permute-start.34 = (bf16[1,128,128]{2,1,0:T(8,128)(2,1)S(1)}, bf16[1,128,128]{2,1,0:T(8,128)(2,1)S(1)}, u32[]{:S(2)}, u32[]{:S(2)}) collective-permute-start(bf16[1,128,128]{2,1,0:T(8,128)(2,1)S(1)} %get-tuple-element.42), channel_id=1, source_target_pairs={{0,1},{1,2},{2,3},{3,0},{4,5},{5,6},{6,7},{7,4},{8,9},{9,10},{10,1... | collective-permute-start | bytes 98312 | tf_op jit(solution)/shard_map/ppermute | solution.py:17
  73.0 5.4 %collective-permute-start.36 = (bf16[1,128,128]{2,1,0:T(8,128)(2,1)S(1)}, bf16[1,128,128]{2,1,0:T(8,128)(2,1)S(1)}, u32[]{:S(2)}, u32[]{:S(2)}) collective-permute-start(bf16[1,128,128]{2,1,0:T(8,128)(2,1)S(1)} %get-tuple-element.12), channel_id=1, source_target_pairs={{0,8},{8,16},{16,24},{24,0},{1,9},{9,17},{17,25},{25,1},{2,10},{10... | collective-permute-start | bytes 98312 | tf_op jit(solution)/shard_map/ppermute | solution.py:17
  73.2 9.0 %collective-permute-start.41 = (bf16[1,128,128]{2,1,0:T(8,128)(2,1)S(1)}, bf16[1,128,128]{2,1,0:T(8,128)(2,1)S(1)}, u32[]{:S(2)}, u32[]{:S(2)}) collective-permute-start(bf16[1,128,128]{2,1,0:T(8,128)(2,1)S(1)} %get-tuple-element.39), channel_id=1, source_target_pairs={{1,0},{2,1},{3,2},{0,3},{5,4},{6,5},{7,6},{4,7},{9,8},{10,9},{11,1... | collective-permute-start | bytes 98312 | tf_op jit(solution)/shard_map/ppermute | solution.py:19
  76.4 5.7 %collective-permute-start.40 = (bf16[1,128,128]{2,1,0:T(8,128)(2,1)S(1)}, bf16[1,128,128]{2,1,0:T(8,128)(2,1)S(1)}, u32[]{:S(2)}, u32[]{:S(2)}) collective-permute-start(bf16[1,128,128]{2,1,0:T(8,128)(2,1)S(1)} %get-tuple-element.40), channel_id=1, source_target_pairs={{0,1},{1,2},{2,3},{3,0},{4,5},{5,6},{6,7},{7,4},{8,9},{9,10},{10,1... | collective-permute-start | bytes 98312 | tf_op jit(solution)/shard_map/ppermute | solution.py:17
  83.9 8.8 %collective-permute-start.47 = (bf16[1,128,128]{2,1,0:T(8,128)(2,1)S(1)}, bf16[1,128,128]{2,1,0:T(8,128)(2,1)S(1)}, u32[]{:S(2)}, u32[]{:S(2)}) collective-permute-start(bf16[1,128,128]{2,1,0:T(8,128)(2,1)S(1)} %get-tuple-element.37), channel_id=1, source_target_pairs={{1,0},{2,1},{3,2},{0,3},{5,4},{6,5},{7,6},{4,7},{9,8},{10,9},{11,1... | collective-permute-start | bytes 98312 | tf_op jit(solution)/shard_map/ppermute | solution.py:19
  86.8 5.9 %collective-permute-start.46 = (bf16[1,128,128]{2,1,0:T(8,128)(2,1)S(1)}, bf16[1,128,128]{2,1,0:T(8,128)(2,1)S(1)}, u32[]{:S(2)}, u32[]{:S(2)}) collective-permute-start(bf16[1,128,128]{2,1,0:T(8,128)(2,1)S(1)} %get-tuple-element.38), channel_id=1, source_target_pairs={{0,1},{1,2},{2,3},{3,0},{4,5},{5,6},{6,7},{7,4},{8,9},{9,10},{10,1... | collective-permute-start | bytes 98312 | tf_op jit(solution)/shard_map/ppermute | solution.py:17
  (31 other events, 152.7 us)
where the time goes:
time: 94 us; the launch traced here: 93.8 us
  starting transfers between devices  51 us (54%)
  waiting for transfers between devices  26.7 us (28%)
  matrix products  10.9 us (12%)
  local copies, waits for them, and re-layouts  3.63 us (4%)
    ppermute x24, starting transfers between devices, padded(): lax.ppermute(head, axis, [((i + 1) % count, i) for i in range(count)])  41.5 us
    ppermute x24, waiting for transfers between devices, padded(): lax.ppermute(tail, axis, [(i, (i + 1) % count) for i in range(count)])  13.9 us
    ppermute x24, waiting for transfers between devices, padded(): lax.ppermute(head, axis, [((i + 1) % count, i) for i in range(count)])  12.8 us
    ppermute x24, starting transfers between devices, padded(): lax.ppermute(tail, axis, [(i, (i + 1) % count) for i in range(count)])  9.48 us
    dot_general x8, matrix products, assemble(): jnp.einsum('fkc,fcl->fkl', onehot_half, across, preferred_element_type=jn...  3.38 us
    dot_general x8, matrix products, schur_part(): product = jnp.dot(rows, res_half, preferred_element_type=jnp.float32)  2.75 us
    dot_general x16, matrix products, to_shared(): jnp.einsum('fkc,fkl->fcl', onehot_half, block, preferred_element_type=jnp...  2.68 us
    dot_general x6, matrix products, dual_part(): product = jnp.dot(rows, mult_half, preferred_element_type=jnp.float32)  2.07 us
  transfers between devices with their start and end apart: 48, of which 22 were waited for; matrix products, arithmetic and copies ran while one was open for 1% of the time, Pallas kernels for 0%

commit v1 on v0

v1 whole, which is shorter than its diff:
```python
import functools

import jax
import jax.numpy as jnp
from jax import lax
from jax.experimental import pallas as pl
from jax.experimental.pallas import tpu as pltpu
from jax.sharding import PartitionSpec as P

ITERS = 4
AXES = ("gx", "gy", "gz")
F32 = jnp.float32
BF16 = jnp.bfloat16


def chebyshev():
    low, high = (0.2, 2.5)
    theta = (high + low) / 2.0
    delta = (high - low) / 2.0
    sigma = theta / delta
    rho = 1.0 / sigma
    factors = [(0.0, 1.0 / theta)]
    for _ in range(1, ITERS):
        rho_new = 1.0 / (2.0 * sigma - rho)
        factors.append((rho_new * rho, 2.0 * rho_new / delta))
        rho = rho_new
    return factors


def dot(a, b):
    return jnp.dot(a, b, preferred_element_type=F32)


def dot_nt(a, b):
    return lax.dot_general(a, b, (((1,), (1,)), ((), ())), preferred_element_type=F32)


def split3(x):
    hi = x.astype(BF16)
    rest = x - hi.astype(F32)
    mid = rest.astype(BF16)
    low = (rest - mid.astype(F32)).astype(BF16)
    return hi, mid, low


def kernel(
    counts, face, order_hbm, intact_hbm, rhs_hbm, schur_hbm, dual_hbm, out_hbm,
    order, intact, rhs, schur, dual, schur_sh, dual_sh, stage, rhs_sh, perm, perm_t,
    acc, vec, mult, update, base, sent, held, load_sem, out_sem, send_sem, recv_sem,
):
    wide = 2 * face
    steps = 2 * ITERS

    def neighbour(f):
        axis = AXES[f // 2]
        count = counts[f // 2]
        shift = count - 1 if f % 2 == 0 else 1
        return {axis: lax.rem(lax.axis_index(axis) + shift, count)}

    near = [neighbour(f) for f in range(6)]

    def remote(e, f):
        return pltpu.make_async_remote_copy(
            src_ref=sent.at[e, f],
            dst_ref=held.at[e, f ^ 1],
            send_sem=send_sem.at[e, f],
            recv_sem=recv_sem.at[e, f ^ 1],
            device_id=near[f],
            device_id_type=pl.DeviceIdType.MESH,
        )

    loads = [
        pltpu.make_async_copy(src, dst, load_sem.at[i])
        for i, (src, dst) in enumerate(
            [(order_hbm, order), (intact_hbm, intact), (rhs_hbm, rhs), (schur_hbm, schur), (dual_hbm, dual)]
        )
    ]
    for load in loads:
        load.start()
    barrier = pltpu.get_barrier_semaphore()
    for f in range(6):
        pl.semaphore_signal(barrier, inc=1, device_id=near[f], device_id_type=pl.DeviceIdType.MESH)

    def rows(g):
        return pl.ds(g * wide, wide)

    def pair(ref, e, g):
        return ref[e, 2 * g : 2 * g + 2].reshape(wide, ref.shape[3])

    def send(e, g, value):
        half = value.astype(BF16)
        for s in range(2):
            f = 2 * g + s
            sent[e, f] = half[s * face : (s + 1) * face]
            remote(e, f).start()

    def receive(e, g):
        for f in (2 * g, 2 * g + 1):
            remote(e, f ^ 1).wait_recv()
        return pair(sent, e, g).astype(F32) + pair(held, e, g).astype(F32)

    loads[0].wait()
    loads[1].wait()
    sub = lax.broadcasted_iota(jnp.int32, (wide, wide), 0)
    lane = lax.broadcasted_iota(jnp.int32, (1, wide), 1)
    offset = jnp.where(lane >= face, face, 0)
    for g in range(3):
        target = order[:, rows(g)] + offset
        match = sub == target
        plain = jnp.where(match, 1.0, 0.0).astype(BF16)
        keep = jnp.broadcast_to(intact[:, rows(g)], (16, wide)).astype(F32).astype(BF16)
        keep_local = dot(keep, plain)[0:1]
        perm[g] = jnp.where(match, keep_local, 0.0).astype(BF16)
    loads[2].wait()
    first = {}
    for g in (2, 1, 0):
        first[g] = dot(perm[g], rhs[rows(g), :].astype(BF16))
    pl.semaphore_wait(barrier, 6)
    for g in (2, 1, 0):
        send(0, g, first[g])

    def conjugate(src, dst, sign):
        for g in range(3):
            stage[rows(g), :] = dot(perm[g], src[rows(g), :]).astype(BF16)
        for g in range(3):
            moved = dot_nt(stage[:, rows(g)], perm[g])
            dst[:, rows(g)] = (moved if sign > 0 else -moved).astype(BF16)

    loads[3].wait()
    conjugate(schur, schur_sh, 1)

    def matvec(e, ops, offset_ref, incoming):
        for g in (0, 1, 2):
            vec[rows(g), :] = incoming(g).astype(BF16)
            if g < 2:
                value = dot(ops[:, rows(g)], vec[rows(g), :])
                if g == 0:
                    acc[...] = value if offset_ref is None else value + offset_ref[...]
                else:
                    acc[...] += value
        for g in (2, 1, 0):
            send(e, g, acc[rows(g), :] + dot(ops[rows(g), rows(2)], vec[rows(2), :]))

    factors = chebyshev()
    for step in range(ITERS):
        e = 2 * step
        if step > 0:
            old, new = factors[step - 1]

            def incoming_multipliers(g, e=e, step=step, old=old, new=new):
                value = new * receive(e - 1, g)
                if step > 1:
                    value = value + old * update[rows(g), :]
                update[rows(g), :] = value
                if step > 1:
                    value = value + mult[rows(g), :]
                mult[rows(g), :] = value
                return value

            matvec(e, dual_sh, rhs_sh, incoming_multipliers)
        matvec(e + 1, schur_sh, None, functools.partial(receive, e))
        if step == 0:
            loads[4].wait()
            conjugate(dual, dual_sh, -1)
            eye = jnp.where(sub == lax.broadcasted_iota(jnp.int32, (wide, wide), 1), 1.0, 0.0).astype(BF16)
            for g in range(3):
                hi, mid, low = split3(rhs[rows(g), :])
                rhs_sh[rows(g), :] = dot(perm[g], hi) + dot(perm[g], mid) + dot(perm[g], low)
                perm_t[g] = dot_nt(eye, perm[g]).astype(BF16)

    last = steps - 1
    old, new = factors[-1]
    for g in range(3):
        hi, mid, low = split3(mult[rows(g), :] + old * update[rows(g), :])
        kept = dot(perm_t[g], hi) + dot(perm_t[g], mid) + dot(perm_t[g], low)
        base[rows(g), :] = kept + new * dot(perm_t[g], pair(sent, last, g))
    stores = []
    for g in range(3):
        for f in (2 * g, 2 * g + 1):
            remote(last, f ^ 1).wait_recv()
        base[rows(g), :] += new * dot(perm_t[g], pair(held, last, g))
        store = pltpu.make_async_copy(base.at[rows(g), :], out_hbm.at[rows(g), :], out_sem.at[g])
        store.start()
        stores.append(store)
    for e in range(steps):
        for f in range(6):
            remote(e, f).wait_send()
    for store in stores:
        store.wait()


def local(counts, dual_ops, schur_ops, local_rhs, ordering, intact):
    size, loads = local_rhs.shape[3:]
    face = size // 6
    wide = 2 * face
    steps = 2 * ITERS
    dual = dual_ops.reshape(size, size)
    schur = schur_ops.reshape(size, size)
    rhs = local_rhs.reshape(size, loads)
    vmem = pltpu.VMEM
    out = pl.pallas_call(
        functools.partial(kernel, counts, face),
        out_shape=jax.ShapeDtypeStruct((size, loads), F32),
        in_specs=[pl.BlockSpec(memory_space=pl.ANY)] * 5,
        out_specs=pl.BlockSpec(memory_space=pl.ANY),
        scratch_shapes=[
            vmem((1, size), jnp.int32),
            vmem((1, size), jnp.int32),
            vmem((size, loads), F32),
            vmem((size, size), BF16),
            vmem((size, size), BF16),
            vmem((size, size), BF16),
            vmem((size, size), BF16),
            vmem((size, size), BF16),
            vmem((size, loads), F32),
            vmem((3, wide, wide), BF16),
            vmem((3, wide, wide), BF16),
            vmem((size, loads), F32),
            vmem((size, loads), BF16),
            vmem((size, loads), F32),
            vmem((size, loads), F32),
            vmem((size, loads), F32),
            vmem((steps, 6, face, loads), BF16),
            vmem((steps, 6, face, loads), BF16),
            pltpu.SemaphoreType.DMA((5,)),
            pltpu.SemaphoreType.DMA((3,)),
            pltpu.SemaphoreType.DMA((steps, 6)),
            pltpu.SemaphoreType.DMA((steps, 6)),
        ],
        compiler_params=pltpu.CompilerParams(
            collective_id=0, has_side_effects=True, vmem_limit_bytes=60 * 1024 * 1024
        ),
        name="feti",
    )(ordering.reshape(1, size), intact.reshape(1, size), rhs, schur, dual)
    return out.reshape(1, 1, 1, size, loads)


def solution(mesh):
    counts = tuple(mesh.shape[axis] for axis in AXES)
    in_specs = (
        P("gx", "gy", "gz", None, None),
        P("gx", "gy", "gz", None, None),
        P("gx", "gy", "gz", None, None),
        P("gx", "gy", "gz", None),
        P("gx", "gy", "gz", None),
    )
    out_specs = P("gx", "gy", "gz", None, None)
    return jax.shard_map(
        functools.partial(local, counts), mesh=mesh, in_specs=in_specs, out_specs=out_specs, check_vma=False
    )
```

time: 94 us -> 43.4 us (0.46)
  starting transfers between devices: 51 us -> 0 us
  Pallas kernels: 0 us -> 41.5 us
  waiting for transfers between devices: 26.7 us -> 0 us
  matrix products: 10.9 us -> 0 us
  local copies, waits for them, and re-layouts: 3.63 us -> 1.77 us
    ppermute x48 -> x0, starting transfers between devices: 51 us -> none  [the longest x24 41.5 us: padded(): lax.ppermute(head, axis, [((i + 1) % count, i) for i in range(count)])]
    pallas_call x0 -> x1, Pallas kernels: none -> 41.5 us  [local(): pl.pallas_call(functools.partial(kernel, counts, face), out_shape=jax.Sha...]
    ppermute x48 -> x0, waiting for transfers between devices: 26.7 us -> none  [the longest x24 13.9 us: padded(): lax.ppermute(tail, axis, [(i, (i + 1) % count) for i in range(count)])]
    dot_general x38 -> x0, matrix products: 10.9 us -> none  [the longest x8 3.38 us: assemble(): jnp.einsum('fkc,fcl->fkl', onehot_half, across, preferred_element_type=jn...]
    convert_element_type x16 -> x0, local copies, waits for them, and re-layouts: 1.86 us -> none  [the longest x8 0.93 us: schur_part(): return product.astype(jnp.bfloat16).reshape(count, FM, loads)]
    unnamed x54 -> x1, local copies, waits for them, and re-layouts: 0.59 us -> 1.77 us
    slice x19 -> x0, local copies, waits for them, and re-layouts: 1.1 us -> none  [the longest x3 0.96 us: rhs_part(): rows = rhs[first * FM:(first + count) * FM]]
  transfers between devices with their start and end apart: 48 -> 0, of which waited for: 22 -> 0; matrix products, arithmetic and copies ran while one was open for 1% -> 0% of each run, Pallas kernels for 0% -> 0%
where the time goes in v1:
time: 43.4 us; the launch traced here: 43.3 us
  Pallas kernels  41.5 us (96%)
  local copies, waits for them, and re-layouts  1.77 us (4%)
    pallas_call x1, Pallas kernels, local(): pl.pallas_call(functools.partial(kernel, counts, face), out_shape=jax.Sha...  41.5 us
    unnamed x1, local copies, waits for them, and re-layouts  1.77 us

profile of v1, /device:TPU:0, one launch (start us, length us, event | category | flops | bytes accessed | tf_op | source)
XLA Modules:
  0.0 43.3 jit_solution(1105276355498284491)
XLA Ops:
  0.0 41.5 %feti.1 = f32[768,128]{1,0:T(8,128)} custom-call(s32[1,768]{1,0:T(1,128)} %bitcast.10, s32[1,768]{1,0:T(1,128)} %bitcast.11, f32[768,128]{1,0:T(8,128)} %bitcast.9, bf16[768,768]{1,0:T(8,128)(2,1)} %bitcast.7, bf16[768,768]{1,0:T(8,128)(2,1)} %bitcast.8), custom_call_target="tpu_custom_call" | custom-call | tf_op jit(solution)/shard_map/feti/pallas_call | solution.py:201
  41.5 1.8 %copy.7 = f32[1,1,1,768,128]{4,3,2,1,0:T(8,128)} copy(f32[1,1,1,768,128]{4,3,2,1,0:T(8,128)} %bitcast.6) | data formatting | bytes 786432

commit v2 on v1

v2 whole, which is shorter than its diff:
```python
import functools

import jax
import jax.numpy as jnp
from jax import lax
from jax.experimental import pallas as pl
from jax.experimental.pallas import tpu as pltpu
from jax.sharding import PartitionSpec as P

ITERS = 4
AXES = ("gx", "gy", "gz")
F32 = jnp.float32
BF16 = jnp.bfloat16


def chebyshev():
    low, high = (0.2, 2.5)
    theta = (high + low) / 2.0
    delta = (high - low) / 2.0
    sigma = theta / delta
    rho = 1.0 / sigma
    factors = [(0.0, 1.0 / theta)]
    for _ in range(1, ITERS):
        rho_new = 1.0 / (2.0 * sigma - rho)
        factors.append((rho_new * rho, 2.0 * rho_new / delta))
        rho = rho_new
    return factors


def dot(a, b):
    return jnp.dot(a, b, preferred_element_type=F32)


def dot_nt(a, b):
    return lax.dot_general(a, b, (((1,), (1,)), ((), ())), preferred_element_type=F32)


def split3(x):
    hi = x.astype(BF16)
    rest = x - hi.astype(F32)
    mid = rest.astype(BF16)
    low = (rest - mid.astype(F32)).astype(BF16)
    return hi, mid, low


def kernel(
    counts, face, order_hbm, intact_hbm, rhs_hbm, schur_hbm, dual_hbm, out,
    order, intact, rhs, schur, dual, schur_sh, dual_sh, stage, rhs_sh, perm, perm_t,
    acc, mult, update, base, sent, held, load_sem, send_sem, recv_sem,
):
    wide = 2 * face
    steps = 2 * ITERS

    def neighbour(f):
        axis = AXES[f // 2]
        count = counts[f // 2]
        shift = count - 1 if f % 2 == 0 else 1
        return {axis: lax.rem(lax.axis_index(axis) + shift, count)}

    near = [neighbour(f) for f in range(6)]

    half = sent.shape[3]

    def remote(e, h, f):
        return pltpu.make_async_remote_copy(
            src_ref=sent.at[e, h, f],
            dst_ref=held.at[e, h, f ^ 1],
            send_sem=send_sem.at[e, h, f],
            recv_sem=recv_sem.at[e, h, f ^ 1],
            device_id=near[f],
            device_id_type=pl.DeviceIdType.MESH,
        )

    loads = [
        pltpu.make_async_copy(src, dst, load_sem.at[i])
        for i, (src, dst) in enumerate(
            [(order_hbm, order), (intact_hbm, intact), (rhs_hbm, rhs), (schur_hbm, schur), (dual_hbm, dual)]
        )
    ]
    for load in loads:
        load.start()
    barrier = pltpu.get_barrier_semaphore()
    for f in range(6):
        pl.semaphore_signal(barrier, inc=1, device_id=near[f], device_id_type=pl.DeviceIdType.MESH)

    def rows(g):
        return pl.ds(g * wide, wide)

    def loads_of(h):
        return pl.ds(h * half, half)

    def pair(ref, e, h, g):
        return jnp.concatenate([ref[e, h, 2 * g], ref[e, h, 2 * g + 1]], axis=1)

    def send(e, h, g, value):
        rounded = value.astype(BF16)
        for s in range(2):
            f = 2 * g + s
            sent[e, h, f] = rounded[:, s * face : (s + 1) * face]
            remote(e, h, f).start()

    def receive(e, h, g):
        for f in (2 * g, 2 * g + 1):
            remote(e, h, f ^ 1).wait_recv()
        return pair(sent, e, h, g).astype(F32) + pair(held, e, h, g).astype(F32)

    loads[0].wait()
    loads[1].wait()
    sub = lax.broadcasted_iota(jnp.int32, (wide, wide), 0)
    lane = lax.broadcasted_iota(jnp.int32, (1, wide), 1)
    offset = jnp.where(lane >= face, face, 0)
    for g in range(3):
        target = order[:, rows(g)] + offset
        match = sub == target
        plain = jnp.where(match, 1.0, 0.0).astype(BF16)
        keep = jnp.broadcast_to(intact[:, rows(g)], (16, wide)).astype(F32).astype(BF16)
        keep_local = dot(keep, plain)[0:1]
        perm[g] = jnp.where(match, keep_local, 0.0).astype(BF16)
    loads[2].wait()
    first = {}
    for g in (2, 1, 0):
        first[g] = jnp.transpose(dot(perm[g], rhs[rows(g), :].astype(BF16)))
    pl.semaphore_wait(barrier, 6)
    for h in range(2):
        for g in (2, 1, 0):
            send(0, h, g, first[g][h * half : (h + 1) * half])

    def conjugate(src, dst, sign):
        for g in range(3):
            stage[rows(g), :] = dot(perm[g], src[rows(g), :]).astype(BF16)
        for g in range(3):
            moved = dot_nt(stage[:, rows(g)], perm[g])
            dst[:, rows(g)] = (moved if sign > 0 else -moved).astype(BF16)

    loads[3].wait()
    conjugate(schur, schur_sh, 1)

    def matvec(e, h, ops, offset_ref, incoming):
        part = loads_of(h)
        for g in range(3):
            vector = incoming(h, g).astype(BF16)
            if g < 2:
                value = dot(vector, ops[rows(g), :])
                if g == 0:
                    acc[part, :] = value if offset_ref is None else value + offset_ref[part, :]
                else:
                    acc[part, :] += value
        for g in (2, 1, 0):
            send(e, h, g, acc[part, rows(g)] + dot(vector, ops[rows(2), rows(g)]))

    factors = chebyshev()
    for step in range(ITERS):
        e = 2 * step
        if step > 0:
            old, new = factors[step - 1]

            def incoming_multipliers(h, g, e=e, step=step, old=old, new=new):
                at = (loads_of(h), rows(g))
                value = new * receive(e - 1, h, g)
                if step > 1:
                    value = value + old * update[at]
                update[at] = value
                if step > 1:
                    value = value + mult[at]
                mult[at] = value
                return value

            for h in range(2):
                matvec(e, h, dual_sh, rhs_sh, incoming_multipliers)
        for h in range(2):
            matvec(e + 1, h, schur_sh, None, functools.partial(receive, e))
        if step == 0:
            loads[4].wait()
            conjugate(dual, dual_sh, -1)
            eye = jnp.where(sub == lax.broadcasted_iota(jnp.int32, (wide, wide), 1), 1.0, 0.0).astype(BF16)
            for g in range(3):
                hi, mid, low = split3(rhs[rows(g), :])
                rhs_sh[:, rows(g)] = jnp.transpose(dot(perm[g], hi) + dot(perm[g], mid) + dot(perm[g], low))
                perm_t[g] = dot_nt(eye, perm[g]).astype(BF16)

    last = steps - 1
    old, new = factors[-1]

    def both(ref, g):
        return jnp.concatenate([pair(ref, last, 0, g), pair(ref, last, 1, g)], axis=0)

    for g in range(3):
        hi, mid, low = split3(mult[:, rows(g)] + old * update[:, rows(g)])
        kept = dot_nt(perm_t[g], hi) + dot_nt(perm_t[g], mid) + dot_nt(perm_t[g], low)
        base[rows(g), :] = kept + new * dot_nt(perm_t[g], both(sent, g))
    for g in range(3):
        for h in range(2):
            for f in (2 * g, 2 * g + 1):
                remote(last, h, f ^ 1).wait_recv()
        out[rows(g), :] = base[rows(g), :] + new * dot_nt(perm_t[g], both(held, g))
    for e in range(steps):
        for h in range(2):
            for f in range(6):
                remote(e, h, f).wait_send()


def local(counts, dual_ops, schur_ops, local_rhs, ordering, intact):
    size, loads = local_rhs.shape[3:]
    face = size // 6
    wide = 2 * face
    steps = 2 * ITERS
    dual = dual_ops.reshape(size, size)
    schur = schur_ops.reshape(size, size)
    rhs = local_rhs.reshape(size, loads)
    vmem = pltpu.VMEM
    out = pl.pallas_call(
        functools.partial(kernel, counts, face),
        out_shape=jax.ShapeDtypeStruct((size, loads), F32),
        in_specs=[pl.BlockSpec(memory_space=pl.ANY)] * 5,
        out_specs=pl.BlockSpec(memory_space=pltpu.VMEM),
        scratch_shapes=[
            vmem((1, size), jnp.int32),
            vmem((1, size), jnp.int32),
            vmem((size, loads), F32),
            vmem((size, size), BF16),
            vmem((size, size), BF16),
            vmem((size, size), BF16),
            vmem((size, size), BF16),
            vmem((size, size), BF16),
            vmem((loads, size), F32),
            vmem((3, wide, wide), BF16),
            vmem((3, wide, wide), BF16),
            vmem((loads, size), F32),
            vmem((loads, size), F32),
            vmem((loads, size), F32),
            vmem((size, loads), F32),
            vmem((steps, 2, 6, loads // 2, face), BF16),
            vmem((steps, 2, 6, loads // 2, face), BF16),
            pltpu.SemaphoreType.DMA((5,)),
            pltpu.SemaphoreType.DMA((steps, 2, 6)),
            pltpu.SemaphoreType.DMA((steps, 2, 6)),
        ],
        compiler_params=pltpu.CompilerParams(
            collective_id=0, has_side_effects=True, vmem_limit_bytes=56000000
        ),
        name="feti",
    )(ordering.reshape(1, size), intact.reshape(1, size), rhs, schur, dual)
    return out.reshape(1, 1, 1, size, loads)


def solution(mesh):
    counts = tuple(mesh.shape[axis] for axis in AXES)
    in_specs = (
        P("gx", "gy", "gz", None, None),
        P("gx", "gy", "gz", None, None),
        P("gx", "gy", "gz", None, None),
        P("gx", "gy", "gz", None),
        P("gx", "gy", "gz", None),
    )
    out_specs = P("gx", "gy", "gz", None, None)
    return jax.shard_map(
        functools.partial(local, counts), mesh=mesh, in_specs=in_specs, out_specs=out_specs, check_vma=False
    )
```

time: 43.4 us -> 41 us (0.945)
  Pallas kernels: 41.5 us -> 38.6 us
    pallas_call x1, Pallas kernels: 41.5 us -> 38.6 us  [local(): pl.pallas_call(functools.partial(kernel, counts, face), out_shape=jax.Sha...]
    unnamed x1 -> x5, local copies, waits for them, and re-layouts: 1.77 us -> 2.12 us
where the time goes in v2:
time: 41 us; the launch traced here: 40.8 us
  Pallas kernels  38.6 us (94%)
  local copies, waits for them, and re-layouts  2.12 us (5%)
    pallas_call x1, Pallas kernels, local(): pl.pallas_call(functools.partial(kernel, counts, face), out_shape=jax.Sha...  38.6 us
    unnamed x5, local copies, waits for them, and re-layouts  2.12 us

profile of v2, /device:TPU:0, one launch (start us, length us, event | category | flops | bytes accessed | tf_op | source)
XLA Modules:
  0.0 40.8 jit_solution(1240648413549444586)
XLA Ops:
  0.0 0.0 copy-start
  0.0 0.7 %copy-done = s32[1,1,1,768]{3,2,1,0:T(1,128)S(1)} copy-done((s32[1,1,1,768]{3,2,1,0:T(1,128)S(1)}, s32[1,1,1,768]{3,2,1,0:T(1,128)}, u32[]{:S(2)}) %copy-start) | copy-done | bytes 3096
  0.7 0.0 copy-start.1
  0.7 0.7 %copy-done.1 = s32[1,1,1,768]{3,2,1,0:T(1,128)S(1)} copy-done((s32[1,1,1,768]{3,2,1,0:T(1,128)S(1)}, s32[1,1,1,768]{3,2,1,0:T(1,128)}, u32[]{:S(2)}) %copy-start.1) | copy-done | bytes 3096
  1.4 38.6 %feti.1 = f32[768,128]{1,0:T(8,128)S(1)} custom-call(s32[1,768]{1,0:T(1,128)S(1)} %bitcast.7, s32[1,768]{1,0:T(1,128)S(1)} %bitcast.8, f32[768,128]{1,0:T(8,128)} %bitcast.11, bf16[768,768]{1,0:T(8,128)(2,1)} %bitcast.9, bf16[768,768]{1,0:T(8,128)(2,1)} %bitcast.10), custom_call_target="tpu_custom_call" | custom-call | tf_op jit(solution)/shard_map/feti/pallas_call | solution.py:211
  40.0 0.7 %copy.7 = f32[1,1,1,768,128]{4,3,2,1,0:T(8,128)} copy(f32[1,1,1,768,128]{4,3,2,1,0:T(8,128)S(1)} %bitcast.6) | data formatting | bytes 786432
Async XLA Ops:
  0.0 0.7 %copy-start = (s32[1,1,1,768]{3,2,1,0:T(1,128)S(1)}, s32[1,1,1,768]{3,2,1,0:T(1,128)}, u32[]{:S(2)}) copy-start(s32[1,1,1,768]{3,2,1,0:T(1,128)} %param.8) | copy-start | bytes 9220
  0.7 0.7 %copy-start.1 = (s32[1,1,1,768]{3,2,1,0:T(1,128)S(1)}, s32[1,1,1,768]{3,2,1,0:T(1,128)}, u32[]{:S(2)}) copy-start(s32[1,1,1,768]{3,2,1,0:T(1,128)} %param.9) | copy-start | bytes 9220

commit v3 on v2

--- a/solution.py
+++ b/solution.py
@@ -99,10 +99,18 @@
             sent[e, h, f] = rounded[:, s * face : (s + 1) * face]
             remote(e, h, f).start()
 
-    def receive(e, h, g):
+    def arrive(e, h, g):
         for f in (2 * g, 2 * g + 1):
             remote(e, h, f ^ 1).wait_recv()
-        return pair(sent, e, h, g).astype(F32) + pair(held, e, h, g).astype(F32)
+        return pair(held, e, h, g).astype(F32)
+
+    def residual(e, h, g):
+        own = pair(sent, e, h, g).astype(F32)
+
+        def finish():
+            return (own + arrive(e, h, g)).astype(BF16), lambda: None
+
+        return finish
 
     loads[0].wait()
     loads[1].wait()
@@ -135,18 +143,22 @@
     loads[3].wait()
     conjugate(schur, schur_sh, 1)
 
-    def matvec(e, h, ops, offset_ref, incoming):
+    def matvec(e, h, ops, offset_ref, begin):
         part = loads_of(h)
-        for g in range(3):
-            vector = incoming(h, g).astype(BF16)
-            if g < 2:
-                value = dot(vector, ops[rows(g), :])
-                if g == 0:
-                    acc[part, :] = value if offset_ref is None else value + offset_ref[part, :]
-                else:
-                    acc[part, :] += value
-        for g in (2, 1, 0):
+        low = []
+        for g in range(2):
+            vector, later = begin(h, g)()
+            low.append(vector)
+            later()
+        value = dot(jnp.concatenate(low, axis=1), ops[pl.ds(0, 2 * wide), :])
+        acc[part, :] = value if offset_ref is None else value + offset_ref[part, :]
+        finish = begin(h, 2)
+        ready, weights = acc[part, rows(2)], ops[rows(2), rows(2)]
+        vector, later = finish()
+        send(e, h, 2, ready + dot(vector, weights))
+        for g in (1, 0):
             send(e, h, g, acc[part, rows(g)] + dot(vector, ops[rows(2), rows(g)]))
+        later()
 
     factors = chebyshev()
     for step in range(ITERS):
@@ -154,21 +166,29 @@
         if step > 0:
             old, new = factors[step - 1]
 
-            def incoming_multipliers(h, g, e=e, step=step, old=old, new=new):
+            def multipliers(h, g, e=e, step=step, old=old, new=new):
                 at = (loads_of(h), rows(g))
-                value = new * receive(e - 1, h, g)
+                change = new * pair(sent, e - 1, h, g).astype(F32)
                 if step > 1:
-                    value = value + old * update[at]
-                update[at] = value
-                if step > 1:
-                    value = value + mult[at]
-                mult[at] = value
-                return value
+                    change = change + old * update[at]
+                total = change if step == 1 else change + mult[at]
+
+                def finish():
+                    rest = new * arrive(e - 1, h, g)
+                    value = total + rest
+
+                    def later():
+                        update[at] = change + rest
+                        mult[at] = value
+
+                    return value.astype(BF16), later
+
+                return finish
 
             for h in range(2):
-                matvec(e, h, dual_sh, rhs_sh, incoming_multipliers)
+                matvec(e, h, dual_sh, rhs_sh, multipliers)
         for h in range(2):
-            matvec(e + 1, h, schur_sh, None, functools.partial(receive, e))
+            matvec(e + 1, h, schur_sh, None, functools.partial(residual, e))
         if step == 0:
             loads[4].wait()
             conjugate(dual, dual_sh, -1)

time: 41 us -> 40.9 us (level)
  no operation moved by 1% of the time
where the time goes in v3:
time: 40.9 us; the launch traced here: 40.7 us
  Pallas kernels  38.6 us (94%)
  local copies, waits for them, and re-layouts  2.12 us (5%)
    pallas_call x1, Pallas kernels, local(): pl.pallas_call(functools.partial(kernel, counts, face), out_shape=jax.Sha...  38.6 us
    unnamed x5, local copies, waits for them, and re-layouts  2.12 us

profile of v3, /device:TPU:0, one launch (start us, length us, event | category | flops | bytes accessed | tf_op | source)
XLA Modules:
  0.0 40.7 jit_solution(580267481131325771)
XLA Ops:
  0.0 0.0 copy-start
  0.0 0.7 %copy-done = s32[1,1,1,768]{3,2,1,0:T(1,128)S(1)} copy-done((s32[1,1,1,768]{3,2,1,0:T(1,128)S(1)}, s32[1,1,1,768]{3,2,1,0:T(1,128)}, u32[]{:S(2)}) %copy-start) | copy-done | bytes 3096
  0.7 0.0 copy-start.1
  0.7 0.7 %copy-done.1 = s32[1,1,1,768]{3,2,1,0:T(1,128)S(1)} copy-done((s32[1,1,1,768]{3,2,1,0:T(1,128)S(1)}, s32[1,1,1,768]{3,2,1,0:T(1,128)}, u32[]{:S(2)}) %copy-start.1) | copy-done | bytes 3096
  1.4 38.6 %feti.1 = f32[768,128]{1,0:T(8,128)S(1)} custom-call(s32[1,768]{1,0:T(1,128)S(1)} %bitcast.7, s32[1,768]{1,0:T(1,128)S(1)} %bitcast.8, f32[768,128]{1,0:T(8,128)} %bitcast.11, bf16[768,768]{1,0:T(8,128)(2,1)} %bitcast.9, bf16[768,768]{1,0:T(8,128)(2,1)} %bitcast.10), custom_call_target="tpu_custom_call" | custom-call | tf_op jit(solution)/shard_map/feti/pallas_call | solution.py:231
  40.0 0.7 %copy.7 = f32[1,1,1,768,128]{4,3,2,1,0:T(8,128)} copy(f32[1,1,1,768,128]{4,3,2,1,0:T(8,128)S(1)} %bitcast.6) | data formatting | bytes 786432
Async XLA Ops:
  0.0 0.7 %copy-start = (s32[1,1,1,768]{3,2,1,0:T(1,128)S(1)}, s32[1,1,1,768]{3,2,1,0:T(1,128)}, u32[]{:S(2)}) copy-start(s32[1,1,1,768]{3,2,1,0:T(1,128)} %param.8) | copy-start | bytes 9220
  0.7 0.7 %copy-start.1 = (s32[1,1,1,768]{3,2,1,0:T(1,128)S(1)}, s32[1,1,1,768]{3,2,1,0:T(1,128)}, u32[]{:S(2)}) copy-start(s32[1,1,1,768]{3,2,1,0:T(1,128)} %param.9) | copy-start | bytes 9220
